TPU v7x, 256 devices: a whole 4x4x8 slice. The times are simulated.
256 devices in a mesh: tm: 8 (over x_hi, y), azim: 32 (over z, x_lo, core).
Axes of the slice: x: 4 (x_hi: 2, x_lo: 2; x = x_hi * 2 + x_lo), y: 4, z: 8, core: 2. Of those that a mesh axis runs over, the one named last changes fastest.
Arguments:
- rotor_coeffs: float32 [64, 2, 32, 16384], P('tm', None, 'azim'), may hold values from -1.5 to 1.5
- mortar_weights: float32 [64, 2, 32, 16384], P('tm', None, 'azim'), may hold values from 0.2 to 1
- block_shifts: int32 [64], P('tm'), may hold values from 0 to 31
- stencil_offsets: int32 [64, 2], P('tm'), may hold values from -1 to 1
- reluctivity: float32 [32, 16384], P('azim'), may hold values from 0.5 to 2
- source: float32 [64, 2, 32, 16384], P('tm', None, 'azim'), may hold values from -3 to 3
Outputs:
- residual: float32 [64, 2, 32, 16384], P('tm', None, 'azim')
All inputs are finite; a program needn't handle non-finite values.
Results may differ from a plain program's by a relative error of at most 0.0001.
Values sent between devices are 32-bit elements; how exact they have to be, the bound alone decides.
A program may use at most 128 MiB of HBM per device.

v0:
```python
import jax
import jax.numpy as jnp
from jax import lax
from jax.sharding import PartitionSpec as P

KC = 64
NT = 64


def shifted(value, axis, steps):
    count = lax.axis_size(axis)
    pairs = [(source, (source + steps) % count) for source in range(count)]
    return lax.ppermute(value, axis, pairs)


def with_halo(value, sides, width):
    for axis, dim in sides:
        devices, length = (lax.axis_size(axis), value.shape[dim])
        up = [(i, (i + 1) % devices) for i in range(devices)]
        down = [(j, i) for i, j in up]
        last = lax.slice_in_dim(value, length - width, length, axis=dim)
        initial = lax.slice_in_dim(value, 0, width, axis=dim)
        before = lax.ppermute(last, axis, up)
        after = lax.ppermute(initial, axis, down)
        value = jnp.concatenate([before, value, after], axis=dim)
    return value


def harmonic_basis(sample_rows, coefficient_count):
    column = jnp.arange(coefficient_count, dtype=jnp.int32)
    harmonic_order = 2 * (column // 2) + 1
    phase_index = harmonic_order[None, :] * (2 * sample_rows[:, None] + 1) % (4 * NT)
    phase_angle = phase_index.astype(jnp.float32) * (jnp.pi / (2 * NT))
    return jnp.where(column[None, :] % 2 == 0, jnp.cos(phase_angle), jnp.sin(phase_angle))


def body(rotor_coeffs, mortar_weights, block_shifts, stencil_offsets, reluctivity, source):
    sample_rows = mortar_weights.shape[0]
    stencil_count = mortar_weights.shape[1]
    full_table = harmonic_basis(jnp.arange(NT, dtype=jnp.int32), KC)
    spread = jnp.einsum(
        "jc,cabp->jabp",
        full_table,
        lax.all_to_all(rotor_coeffs, "tm", split_axis=3, concat_axis=0, tiled=True),
        precision=lax.Precision.HIGHEST,
    )
    samples = lax.all_to_all(spread, "tm", split_axis=0, concat_axis=3, tiled=True)
    turned = samples
    for bit_level in range((lax.axis_size("azim") - 1).bit_length()):
        moved = shifted(turned, "azim", 1 << bit_level)
        chosen = block_shifts >> bit_level & 1 == 1
        turned = jnp.where(chosen[:, None, None, None], moved, turned)
    padded = with_halo(turned, (("azim", 2),), 1)
    airgap_field = jnp.zeros_like(samples)
    for stencil_entry in range(stencil_count):
        pick_index = stencil_offsets[:, stencil_entry] + 1
        neighbour = jnp.zeros_like(samples)
        for position in range(3):
            neighbour = neighbour + jnp.where(
                (pick_index == position)[:, None, None, None],
                padded[:, :, position : position + 1],
                0.0,
            )
        airgap_field = airgap_field + mortar_weights[:, stencil_entry][:, None] * neighbour
    square = jnp.sum(airgap_field * airgap_field, axis=1, keepdims=True)
    field_flux = reluctivity[None, None] * (1.0 + square / (1.0 + square)) * airgap_field
    first_sample = lax.axis_index("tm") * sample_rows
    local_table = harmonic_basis(first_sample + jnp.arange(sample_rows, dtype=jnp.int32), KC) * (
        2.0 / NT
    )
    summed = lax.psum_scatter(
        jnp.einsum("jc,jabp->cabp", local_table, field_flux, precision=lax.Precision.HIGHEST),
        "tm",
        scatter_dimension=0,
        tiled=True,
    )
    return summed - source


def solution(mesh):
    in_specs = (
        P("tm", None, "azim", None),
        P("tm", None, "azim", None),
        P("tm"),
        P("tm", None),
        P("azim", None),
        P("tm", None, "azim", None),
    )
    out_specs = P("tm", None, "azim", None)
    return jax.shard_map(body, mesh=mesh, in_specs=in_specs, out_specs=out_specs, check_vma=False)
```

profile of v0, /device:TPU:1, one launch (start us, length us, event | category | flops | bytes accessed | tf_op | source)
XLA Modules:
  0.0 525.8 jit_solution(4220196497033002725)
XLA Ops:
  6.5 17.4 %copy.23 = f32[8,2,1,16384]{0,1,2,3:T(2,128)} copy(f32[8,2,1,16384]{3,2,1,0:T(1,128)} %param.6) | data formatting | bytes 2097152 | tf_op args[0]
  23.9 29.0 %reshape.168 = f32[8,1,32768]{2,1,0:T(1,128)} reshape(f32[16384,1,2,8]{3,2,1,0:T(2,128)} %bitcast.44) | data formatting | bytes 2097152
  52.9 7.5 %all-to-all-start = ((f32[8,1,32768]{2,1,0:T(1,128)}), f32[8,1,32768]{2,1,0:T(1,128)S(1)}, u32[]{:S(2)}, u32[]{:S(2)}) async-start(f32[8,1,32768]{2,1,0:T(1,128)} %reshape.168), calls=%async_computation | async-start | bytes 2097152 | tf_op jit(solution)/shard_map/all_to_all | solution.py:44
  60.4 0.2 reduce-scatter.2.cloned.1.call-start
  60.6 13.9 %all-to-all-done = f32[8,1,32768]{2,1,0:T(1,128)S(1)} async-done(((f32[8,1,32768]{2,1,0:T(1,128)}), f32[8,1,32768]{2,1,0:T(1,128)S(1)}, u32[]{:S(2)}, u32[]{:S(2)}) %all-to-all-start) | async-done | bytes 1048608 | tf_op jit(solution)/shard_map/all_to_all | solution.py:44
  74.5 0.5 broadcast.282
  75.0 3.1 reduce.1
  78.2 32.1 %reshape.169 = f32[16384,1,2,8]{3,2,1,0:T(2,128)} reshape(f32[8,32768]{1,0:T(8,128)S(1)} %reduce.1) | data formatting | bytes 2097152
  110.3 20.2 %copy.31 = f32[8,2,1,8,2048]{4,0,3,1,2:T(8,128)S(1)} copy(f32[8,2,1,8,2048]{0,1,4,3,2:T(2,128)} %bitcast.43) | data formatting | bytes 2097152 | tf_op jit(solution)/shard_map/all_to_all | solution.py:44
  130.5 1.3 convolution_bitcast_fusion.1
  131.8 0.8 copy.26
  132.6 21.4 %all_to_all.33 = f32[64,2,1,2048]{3,1,2,0:T(2,128)S(1)} all-to-all(f32[64,2,1,2048]{3,1,2,0:T(2,128)S(1)} %copy.26), channel_id=1, replica_groups=mesh['tm'=8,'azim'=32] {'tm'}, dimensions={0} | all-to-all | bytes 2097152 | tf_op jit(solution)/shard_map/all_to_all | solution.py:47
  154.0 0.6 copy.27
  154.6 2.8 collective-permute-start
  157.4 11.7 %collective-permute-done = f32[8,2,1,16384]{3,0,1,2:T(8,128)S(1)} collective-permute-done((f32[8,2,1,16384]{3,0,1,2:T(8,128)S(1)}, f32[8,2,1,16384]{3,0,1,2:T(8,128)S(1)}, u32[]{:S(2)}, u32[]{:S(2)}) %collective-permute-start) | collective-permute-done | bytes 1048608 | tf_op jit(solution)/shard_map/ppermute | solution.py:13
  169.3 2.5 collective-permute-start.1
  171.8 20.8 %collective-permute-done.1 = f32[8,2,1,16384]{3,0,1,2:T(8,128)S(1)} collective-permute-done((f32[8,2,1,16384]{3,0,1,2:T(8,128)S(1)}, f32[8,2,1,16384]{3,0,1,2:T(8,128)S(1)}, u32[]{:S(2)}, u32[]{:S(2)}) %collective-permute-start.1) | collective-permute-done | bytes 1048608 | tf_op jit(solution)/shard_map/ppermute | solution.py:13
  192.9 3.0 collective-permute-start.2
  195.9 21.3 %collective-permute-done.2 = f32[8,2,1,16384]{3,0,1,2:T(8,128)S(1)} collective-permute-done((f32[8,2,1,16384]{3,0,1,2:T(8,128)S(1)}, f32[8,2,1,16384]{3,0,1,2:T(8,128)S(1)}, u32[]{:S(2)}, u32[]{:S(2)}) %collective-permute-start.2) | collective-permute-done | bytes 1048608 | tf_op jit(solution)/shard_map/ppermute | solution.py:13
  217.3 5.8 %collective-permute-start.3 = (f32[8,2,1,16384]{3,0,1,2:T(8,128)S(1)}, f32[8,2,1,16384]{3,0,1,2:T(8,128)S(1)}, u32[]{:S(2)}, u32[]{:S(2)}) collective-permute-start(f32[8,2,1,16384]{3,0,1,2:T(8,128)S(1)} %broadcast_select_fusion.2), channel_id=1, source_target_pairs={{0,8},{1,9},{2,10},{3,11},{4,12},{5,13},{6,14},{7,15},{8,16},{9,17... | collective-permute-start | bytes 3145736 | tf_op jit(solution)/shard_map/ppermute | solution.py:13
  223.2 42.9 %collective-permute-done.3 = f32[8,2,1,16384]{3,0,1,2:T(8,128)S(1)} collective-permute-done((f32[8,2,1,16384]{3,0,1,2:T(8,128)S(1)}, f32[8,2,1,16384]{3,0,1,2:T(8,128)S(1)}, u32[]{:S(2)}, u32[]{:S(2)}) %collective-permute-start.3) | collective-permute-done | bytes 1048608 | tf_op jit(solution)/shard_map/ppermute | solution.py:13
  266.2 1.4 collective-permute-start.4
  267.8 25.5 %collective-permute-done.4 = f32[8,2,1,16384]{3,0,1,2:T(8,128)S(1)} collective-permute-done((f32[8,2,1,16384]{3,0,1,2:T(8,128)S(1)}, f32[8,2,1,16384]{3,0,1,2:T(8,128)S(1)}, u32[]{:S(2)}, u32[]{:S(2)}) %collective-permute-start.4) | collective-permute-done | bytes 1048608 | tf_op jit(solution)/shard_map/ppermute | solution.py:13
  293.4 3.3 collective-permute-start.6
  296.7 3.6 collective-permute-start.5
  300.3 0.6 copy_bitcast_fusion
  301.0 11.8 %collective-permute-done.6 = f32[8,2,1,16384]{3,0,1,2:T(8,128)} collective-permute-done((f32[8,2,1,16384]{3,0,1,2:T(8,128)S(1)}, f32[8,2,1,16384]{3,0,1,2:T(8,128)}, u32[]{:S(2)}, u32[]{:S(2)}) %collective-permute-start.6) | collective-permute-done | bytes 1048608 | tf_op jit(solution)/shard_map/ppermute | solution.py:24
  312.8 2.2 multiply_reduce_fusion
  315.1 9.2 %convolution_bitcast_fusion = f32[64,2,1,16384]{3,0,1,2:T(8,128)} fusion(f32[8,2,1,16384]{3,0,1,2:T(8,128)S(1)} %get-tuple-element.6, f32[8,16384]{1,0:T(8,128)S(1)} %fusion.4, s32[8]{0:T(128)S(1)} %multiply_add_fusion.2, s32[64]{0:T(128)S(1)} %get-tuple-element.20, pred[64]{0:T(512)(128)(4,1)S(1)} %fusion.44), kind=kOutput, calls=%fused_computation | convolution fusion | flops 201596928 | bytes 9961824 | tf_op jit(solution)/shard_map/jc,jabp->cabp/dot_general | solution.py:72
  324.3 190.7 %reduce-scatter.2.cloned.1.call-done = f32[8,2,1,16384]{3,0,1,2:T(8,128)} async-done(((f32[64,2,1,16384]{3,0,1,2:T(8,128)}), f32[8,2,1,16384]{3,0,1,2:T(8,128)}) %reduce-scatter.2.cloned.1.call-update) | async-done | bytes 1048592 | tf_op jit(solution)/shard_map/reduce_scatter | solution.py:71
  515.1 1.9 copy_subtract_fusion
  516.9 2.0 copy.29
  (24 shorter events, 1.1 us)
Async XLA Ops:
  52.9 21.7 %all-to-all-start = ((f32[8,1,32768]{2,1,0:T(1,128)}), f32[8,1,32768]{2,1,0:T(1,128)S(1)}, u32[]{:S(2)}, u32[]{:S(2)}) async-start(f32[8,1,32768]{2,1,0:T(1,128)} %reshape.168), calls=%async_computation | async-start | bytes 2097152 | tf_op jit(solution)/shard_map/all_to_all | solution.py:44
  60.4 454.7 %reduce-scatter.2.cloned.1.call-start = ((), (), s32[]{:S(2)}) async-start(), calls=%async_computation.3 | async-start | bytes 9437184 | tf_op jit(solution)/shard_map/reduce_scatter | solution.py:71
  110.3 47.1 %copy-start.4 = (s32[8]{0:T(128)S(1)}, s32[8]{0:T(128)}, u32[]{:S(2)}) copy-start(s32[8]{0:T(128)} %param.8) | copy-start | bytes 100
  110.3 157.4 %copy-start.1 = (f32[8,2,1,16384]{3,2,1,0:T(1,128)S(1)}, f32[8,2,1,16384]{3,2,1,0:T(1,128)}, u32[]{:S(2)}) copy-start(f32[8,2,1,16384]{3,2,1,0:T(1,128)} %param.7) | copy-start | bytes 3145732
  130.5 170.4 %copy-start.3 = (s32[8,2]{0,1:T(2,128)S(1)}, s32[8,2]{0,1:T(2,128)}, u32[]{:S(2)}) copy-start(s32[8,2]{0,1:T(2,128)} %param.9) | copy-start | bytes 196
  130.5 184.5 %copy-start.2 = (f32[1,16384]{1,0:T(1,128)S(1)}, f32[1,16384]{1,0:T(1,128)}, u32[]{:S(2)}) copy-start(f32[1,16384]{1,0:T(1,128)} %param.10) | copy-start | bytes 196612
  154.6 14.6 %collective-permute-start = (f32[8,2,1,16384]{3,0,1,2:T(8,128)S(1)}, f32[8,2,1,16384]{3,0,1,2:T(8,128)S(1)}, u32[]{:S(2)}, u32[]{:S(2)}) collective-permute-start(f32[8,2,1,16384]{3,0,1,2:T(8,128)S(1)} %bitcast.45), channel_id=1, source_target_pairs={{0,1},{1,2},{2,3},{3,4},{4,5},{5,6},{6,7},{7,8},{8,9},{9,10},{10,1... | collective-permute-start | bytes 3145736 | tf_op jit(solution)/shard_map/ppermute | solution.py:13
  169.3 23.3 %collective-permute-start.1 = (f32[8,2,1,16384]{3,0,1,2:T(8,128)S(1)}, f32[8,2,1,16384]{3,0,1,2:T(8,128)S(1)}, u32[]{:S(2)}, u32[]{:S(2)}) collective-permute-start(f32[8,2,1,16384]{3,0,1,2:T(8,128)S(1)} %broadcast_select_fusion), channel_id=1, source_target_pairs={{0,2},{1,3},{2,4},{3,5},{4,6},{5,7},{6,8},{7,9},{8,10},{9,11},{10,... | collective-permute-start | bytes 3145736 | tf_op jit(solution)/shard_map/ppermute | solution.py:13
  192.9 24.3 %collective-permute-start.2 = (f32[8,2,1,16384]{3,0,1,2:T(8,128)S(1)}, f32[8,2,1,16384]{3,0,1,2:T(8,128)S(1)}, u32[]{:S(2)}, u32[]{:S(2)}) collective-permute-start(f32[8,2,1,16384]{3,0,1,2:T(8,128)S(1)} %broadcast_select_fusion.1), channel_id=1, source_target_pairs={{0,4},{1,5},{2,6},{3,7},{4,8},{5,9},{6,10},{7,11},{8,12},{9,13},{1... | collective-permute-start | bytes 3145736 | tf_op jit(solution)/shard_map/ppermute | solution.py:13
  217.3 48.7 %collective-permute-start.3 = (f32[8,2,1,16384]{3,0,1,2:T(8,128)S(1)}, f32[8,2,1,16384]{3,0,1,2:T(8,128)S(1)}, u32[]{:S(2)}, u32[]{:S(2)}) collective-permute-start(f32[8,2,1,16384]{3,0,1,2:T(8,128)S(1)} %broadcast_select_fusion.2), channel_id=1, source_target_pairs={{0,8},{1,9},{2,10},{3,11},{4,12},{5,13},{6,14},{7,15},{8,16},{9,17... | collective-permute-start | bytes 3145736 | tf_op jit(solution)/shard_map/ppermute | solution.py:13
  266.2 248.8 %copy-start = (f32[8,2,1,16384]{3,2,1,0:T(1,128)S(1)}, f32[8,2,1,16384]{3,2,1,0:T(1,128)}, u32[]{:S(2)}) copy-start(f32[8,2,1,16384]{3,2,1,0:T(1,128)} %param.11) | copy-start | bytes 3145732
  266.2 27.0 %collective-permute-start.4 = (f32[8,2,1,16384]{3,0,1,2:T(8,128)S(1)}, f32[8,2,1,16384]{3,0,1,2:T(8,128)S(1)}, u32[]{:S(2)}, u32[]{:S(2)}) collective-permute-start(f32[8,2,1,16384]{3,0,1,2:T(8,128)S(1)} %broadcast_select_fusion.3), channel_id=1, source_target_pairs={{0,16},{1,17},{2,18},{3,19},{4,20},{5,21},{6,22},{7,23},{8,24},{9,... | collective-permute-start | bytes 3145736 | tf_op jit(solution)/shard_map/ppermute | solution.py:13
  293.4 19.4 %collective-permute-start.6 = (f32[8,2,1,16384]{3,0,1,2:T(8,128)S(1)}, f32[8,2,1,16384]{3,0,1,2:T(8,128)}, u32[]{:S(2)}, u32[]{:S(2)}) collective-permute-start(f32[8,2,1,16384]{3,0,1,2:T(8,128)S(1)} %broadcast_select_fusion.4), channel_id=1, source_target_pairs={{1,0},{2,1},{3,2},{4,3},{5,4},{6,5},{7,6},{8,7},{9,8},{10,9},{11,1... | collective-permute-start | bytes 3145736 | tf_op jit(solution)/shard_map/ppermute | solution.py:24
  296.7 16.1 %collective-permute-start.5 = (f32[8,2,1,16384]{3,0,1,2:T(8,128)S(1)}, f32[8,2,1,16384]{3,0,1,2:T(8,128)}, u32[]{:S(2)}, u32[]{:S(2)}) collective-permute-start(f32[8,2,1,16384]{3,0,1,2:T(8,128)S(1)} %broadcast_select_fusion.4), channel_id=1, source_target_pairs={{0,1},{1,2},{2,3},{3,4},{4,5},{5,6},{6,7},{7,8},{8,9},{9,10},{10,1... | collective-permute-start | bytes 3145736 | tf_op jit(solution)/shard_map/ppermute | solution.py:23
Sparse Core Ops, SparseCore 0:
  324.5 190.5 reduce-scatter.1
where the time goes:
time: 528 us; the launch traced here: 526 us
  waiting for transfers between devices  339 us (64%)
  local copies, waits for them, and re-layouts  103 us (20%)
  starting transfers between devices  30.2 us (6%)
  blocking collectives  21.4 us (4%)
  between operations  13.5 us (3%)
  matrix products  10.4 us (2%)
  other arithmetic  8.16 us (2%)
    reduce_scatter x1, waiting for transfers between devices, body(): lax.psum_scatter(jnp.einsum('jc,jabp->cabp', local_table, field_flux, pre...  191 us
    ppermute x5, waiting for transfers between devices, shifted(): return lax.ppermute(value, axis, pairs)  122 us
    unnamed x14, local copies, waits for them, and re-layouts  79.1 us
    all_to_all x1, blocking collectives, body(): lax.all_to_all(spread, 'tm', split_axis=0, concat_axis=3, tiled=True)  21.4 us
    all_to_all x2, local copies, waits for them, and re-layouts, body(): lax.all_to_all(rotor_coeffs, 'tm', split_axis=3, concat_axis=0, tiled=True)  20.7 us
    ppermute x5, starting transfers between devices, shifted(): return lax.ppermute(value, axis, pairs)  15.6 us
    all_to_all x1, waiting for transfers between devices, body(): lax.all_to_all(rotor_coeffs, 'tm', split_axis=3, concat_axis=0, tiled=True)  13.9 us
    ppermute x1, waiting for transfers between devices, with_halo(): after = lax.ppermute(initial, axis, down)  11.8 us
  transfers between devices with their start and end apart: 9, of which 8 were waited for; matrix products, arithmetic and copies ran while one was open for 0% of the time, Pallas kernels for 0%

commit v1 on v0

--- a/solution.py
+++ b/solution.py
@@ -41,7 +41,12 @@
     spread = jnp.einsum(
         "jc,cabp->jabp",
         full_table,
-        lax.all_to_all(rotor_coeffs, "tm", split_axis=3, concat_axis=0, tiled=True),
+        jnp.concatenate(
+            lax.all_to_all(
+                jnp.stack(jnp.split(rotor_coeffs, lax.axis_size("tm"), axis=3)), "tm", 0, 0
+            ),
+            axis=0,
+        ),
         precision=lax.Precision.HIGHEST,
     )
     samples = lax.all_to_all(spread, "tm", split_axis=0, concat_axis=3, tiled=True)

time: 528 us -> 436 us (0.83)
  local copies, waits for them, and re-layouts: 103 us -> 16.7 us
    unnamed x14 -> x18, local copies, waits for them, and re-layouts: 79.1 us -> 11.6 us
    reduce_scatter x1, waiting for transfers between devices: 191 us -> 169 us  [body(): lax.psum_scatter(jnp.einsum('jc,jabp->cabp', local_table, field_flux, pre...]
    ppermute x1, waiting for transfers between devices: 0.01 us -> 20.9 us  [with_halo(): before = lax.ppermute(last, axis, up)]
    all_to_all x2 -> x0, local copies, waits for them, and re-layouts: 20.7 us -> none  [body(): lax.all_to_all(rotor_coeffs, 'tm', split_axis=3, concat_axis=0, tiled=True)]
  transfers between devices with their start and end apart: 9 -> 9, of which waited for: 8 -> 9; matrix products, arithmetic and copies ran while one was open for 0% -> 0% of each run, Pallas kernels for 0% -> 0%
where the time goes in v1:
time: 436 us; the launch traced here: 435 us
  waiting for transfers between devices  339 us (78%)
  starting transfers between devices  29.4 us (7%)
  blocking collectives  21.5 us (5%)
  local copies, waits for them, and re-layouts  16.7 us (4%)
  between operations  13.5 us (3%)
  matrix products  10.9 us (2%)
  other arithmetic  4.71 us (1%)
    reduce_scatter x1, waiting for transfers between devices, body(): lax.psum_scatter(jnp.einsum('jc,jabp->cabp', local_table, field_flux, pre...  169 us
    ppermute x5, waiting for transfers between devices, shifted(): return lax.ppermute(value, axis, pairs)  123 us
    all_to_all x1, blocking collectives, body(): lax.all_to_all(spread, 'tm', split_axis=0, concat_axis=3, tiled=True)  21.5 us
    ppermute x1, waiting for transfers between devices, with_halo(): before = lax.ppermute(last, axis, up)  20.9 us
    ppermute x5, starting transfers between devices, shifted(): return lax.ppermute(value, axis, pairs)  15.3 us
    all_to_all x1, waiting for transfers between devices, body(): lax.all_to_all(jnp.stack(jnp.split(rotor_coeffs, lax.axis_size('tm'), axi...  14.1 us
    unnamed x18, local copies, waits for them, and re-layouts  11.6 us
    ppermute x1, waiting for transfers between devices, with_halo(): after = lax.ppermute(initial, axis, down)  11.6 us
  transfers between devices with their start and end apart: 9, of which 9 were waited for; matrix products, arithmetic and copies ran while one was open for 0% of the time, Pallas kernels for 0%

profile of v1, /device:TPU:1, one launch (start us, length us, event | category | flops | bytes accessed | tf_op | source)
XLA Modules:
  0.0 435.4 jit_solution(369877964588462634)
XLA Ops:
  6.5 1.6 bitcast_dynamic-update-slice_fusion.7
  8.1 1.6 bitcast_dynamic-update-slice_fusion.6
  9.7 1.6 bitcast_dynamic-update-slice_fusion.5
  11.3 1.6 bitcast_dynamic-update-slice_fusion.4
  12.8 1.6 bitcast_dynamic-update-slice_fusion.3
  14.4 1.6 bitcast_dynamic-update-slice_fusion.2
  16.0 1.6 bitcast_dynamic-update-slice_fusion.1
  17.5 1.6 bitcast_dynamic-update-slice_fusion
  19.1 7.5 %all-to-all-start = ((f32[8,8,2,1,2048]{4,3,2,1,0:T(1,128)}), f32[8,8,2,1,2048]{4,3,2,1,0:T(1,128)S(1)}, u32[]{:S(2)}, u32[]{:S(2)}) async-start(f32[8,8,2,1,2048]{4,3,2,1,0:T(1,128)} %bitcast_dynamic-update-slice_fusion), calls=%async_computation | async-start | bytes 2097152 | tf_op jit(solution)/shard_map/all_to_all | solution.py:45
  26.6 14.1 %all-to-all-done = f32[8,8,2,1,2048]{4,3,2,1,0:T(1,128)S(1)} async-done(((f32[8,8,2,1,2048]{4,3,2,1,0:T(1,128)}), f32[8,8,2,1,2048]{4,3,2,1,0:T(1,128)S(1)}, u32[]{:S(2)}, u32[]{:S(2)}) %all-to-all-start) | async-done | bytes 1048608 | tf_op jit(solution)/shard_map/all_to_all | solution.py:45
  40.8 1.8 convolution_bitcast_fusion.1
  42.5 0.8 copy.11
  43.4 21.5 %all_to_all.23 = f32[64,2,1,2048]{3,1,2,0:T(2,128)S(1)} all-to-all(f32[64,2,1,2048]{3,1,2,0:T(2,128)S(1)} %copy.11), channel_id=1, replica_groups=mesh['tm'=8,'azim'=32] {'tm'}, dimensions={0} | all-to-all | bytes 2097152 | tf_op jit(solution)/shard_map/all_to_all | solution.py:52
  65.5 2.8 collective-permute-start
  68.3 11.7 %collective-permute-done = f32[8,2,1,16384]{3,0,1,2:T(8,128)S(1)} collective-permute-done((f32[8,2,1,16384]{3,0,1,2:T(8,128)S(1)}, f32[8,2,1,16384]{3,0,1,2:T(8,128)S(1)}, u32[]{:S(2)}, u32[]{:S(2)}) %collective-permute-start) | collective-permute-done | bytes 1048608 | tf_op jit(solution)/shard_map/ppermute | solution.py:13
  80.2 2.5 collective-permute-start.1
  82.7 20.8 %collective-permute-done.1 = f32[8,2,1,16384]{3,0,1,2:T(8,128)S(1)} collective-permute-done((f32[8,2,1,16384]{3,0,1,2:T(8,128)S(1)}, f32[8,2,1,16384]{3,0,1,2:T(8,128)S(1)}, u32[]{:S(2)}, u32[]{:S(2)}) %collective-permute-start.1) | collective-permute-done | bytes 1048608 | tf_op jit(solution)/shard_map/ppermute | solution.py:13
  103.7 3.0 collective-permute-start.2
  106.7 21.3 %collective-permute-done.2 = f32[8,2,1,16384]{3,0,1,2:T(8,128)S(1)} collective-permute-done((f32[8,2,1,16384]{3,0,1,2:T(8,128)S(1)}, f32[8,2,1,16384]{3,0,1,2:T(8,128)S(1)}, u32[]{:S(2)}, u32[]{:S(2)}) %collective-permute-start.2) | collective-permute-done | bytes 1048608 | tf_op jit(solution)/shard_map/ppermute | solution.py:13
  128.2 5.8 %collective-permute-start.3 = (f32[8,2,1,16384]{3,0,1,2:T(8,128)S(1)}, f32[8,2,1,16384]{3,0,1,2:T(8,128)S(1)}, u32[]{:S(2)}, u32[]{:S(2)}) collective-permute-start(f32[8,2,1,16384]{3,0,1,2:T(8,128)S(1)} %broadcast_select_fusion.2), channel_id=1, source_target_pairs={{0,8},{1,9},{2,10},{3,11},{4,12},{5,13},{6,14},{7,15},{8,16},{9,17... | collective-permute-start | bytes 3145736 | tf_op jit(solution)/shard_map/ppermute | solution.py:13
  134.1 42.9 %collective-permute-done.3 = f32[8,2,1,16384]{3,0,1,2:T(8,128)S(1)} collective-permute-done((f32[8,2,1,16384]{3,0,1,2:T(8,128)S(1)}, f32[8,2,1,16384]{3,0,1,2:T(8,128)S(1)}, u32[]{:S(2)}, u32[]{:S(2)}) %collective-permute-start.3) | collective-permute-done | bytes 1048608 | tf_op jit(solution)/shard_map/ppermute | solution.py:13
  177.2 1.2 collective-permute-start.4
  178.4 25.9 %collective-permute-done.4 = f32[8,2,1,16384]{3,0,1,2:T(8,128)S(1)} collective-permute-done((f32[8,2,1,16384]{3,0,1,2:T(8,128)S(1)}, f32[8,2,1,16384]{3,0,1,2:T(8,128)S(1)}, u32[]{:S(2)}, u32[]{:S(2)}) %collective-permute-start.4) | collective-permute-done | bytes 1048608 | tf_op jit(solution)/shard_map/ppermute | solution.py:13
  204.5 3.0 collective-permute-start.6
  207.6 3.6 collective-permute-start.5
  211.8 11.6 %collective-permute-done.6 = f32[8,2,1,16384]{3,0,1,2:T(8,128)S(1)} collective-permute-done((f32[8,2,1,16384]{3,0,1,2:T(8,128)S(1)}, f32[8,2,1,16384]{3,0,1,2:T(8,128)S(1)}, u32[]{:S(2)}, u32[]{:S(2)}) %collective-permute-start.6) | collective-permute-done | bytes 1048608 | tf_op jit(solution)/shard_map/ppermute | solution.py:24
  223.3 20.9 %collective-permute-done.5 = f32[8,2,1,16384]{3,0,1,2:T(8,128)} collective-permute-done((f32[8,2,1,16384]{3,0,1,2:T(8,128)S(1)}, f32[8,2,1,16384]{3,0,1,2:T(8,128)}, u32[]{:S(2)}, u32[]{:S(2)}) %collective-permute-start.5) | collective-permute-done | bytes 1048608 | tf_op jit(solution)/shard_map/ppermute | solution.py:23
  244.2 1.9 multiply_reduce_fusion
  246.2 9.2 %convolution_bitcast_fusion = f32[64,2,1,16384]{3,0,1,2:T(8,128)} fusion(f32[8,2,1,16384]{3,0,1,2:T(8,128)S(1)} %get-tuple-element.6, f32[8,16384]{1,0:T(8,128)S(1)} %fusion.5, s32[8]{0:T(128)S(1)} %multiply_add_fusion.2, s32[64]{0:T(128)S(1)} %get-tuple-element.20, pred[64]{0:T(512)(128)(4,1)S(1)} %fusion.45), kind=kOutput, calls=%fused_computation | convolution fusion | flops 201596928 | bytes 9961824 | tf_op jit(solution)/shard_map/jc,jabp->cabp/dot_general | solution.py:77
  255.4 169.3 %reduce-scatter.2.cloned.1.call-done = f32[8,2,1,16384]{3,0,1,2:T(8,128)} async-done(((f32[64,2,1,16384]{3,0,1,2:T(8,128)}), f32[8,2,1,16384]{3,0,1,2:T(8,128)}) %reduce-scatter.2.cloned.1.call-update) | async-done | bytes 1048592 | tf_op jit(solution)/shard_map/reduce_scatter | solution.py:76
  424.7 1.9 copy_subtract_fusion
  426.5 2.0 copy.14
  (26 shorter events, 2.4 us)
Async XLA Ops:
  6.5 61.8 %copy-start.4 = (s32[8]{0:T(128)S(1)}, s32[8]{0:T(128)}, u32[]{:S(2)}) copy-start(s32[8]{0:T(128)} %param.8) | copy-start | bytes 100
  19.1 21.7 %all-to-all-start = ((f32[8,8,2,1,2048]{4,3,2,1,0:T(1,128)}), f32[8,8,2,1,2048]{4,3,2,1,0:T(1,128)S(1)}, u32[]{:S(2)}, u32[]{:S(2)}) async-start(f32[8,8,2,1,2048]{4,3,2,1,0:T(1,128)} %bitcast_dynamic-update-slice_fusion), calls=%async_computation | async-start | bytes 2097152 | tf_op jit(solution)/shard_map/all_to_all | solution.py:45
  26.6 398.1 %reduce-scatter.2.cloned.1.call-start = ((), (), s32[]{:S(2)}) async-start(), calls=%async_computation.3 | async-start | bytes 9437184 | tf_op jit(solution)/shard_map/reduce_scatter | solution.py:76
  43.4 135.0 %copy-start.1 = (f32[8,2,1,16384]{3,2,1,0:T(1,128)S(1)}, f32[8,2,1,16384]{3,2,1,0:T(1,128)}, u32[]{:S(2)}) copy-start(f32[8,2,1,16384]{3,2,1,0:T(1,128)} %param.7) | copy-start | bytes 3145732
  65.5 14.6 %collective-permute-start = (f32[8,2,1,16384]{3,0,1,2:T(8,128)S(1)}, f32[8,2,1,16384]{3,0,1,2:T(8,128)S(1)}, u32[]{:S(2)}, u32[]{:S(2)}) collective-permute-start(f32[8,2,1,16384]{3,0,1,2:T(8,128)S(1)} %bitcast.53), channel_id=1, source_target_pairs={{0,1},{1,2},{2,3},{3,4},{4,5},{5,6},{6,7},{7,8},{8,9},{9,10},{10,1... | collective-permute-start | bytes 3145736 | tf_op jit(solution)/shard_map/ppermute | solution.py:13
  80.2 23.3 %collective-permute-start.1 = (f32[8,2,1,16384]{3,0,1,2:T(8,128)S(1)}, f32[8,2,1,16384]{3,0,1,2:T(8,128)S(1)}, u32[]{:S(2)}, u32[]{:S(2)}) collective-permute-start(f32[8,2,1,16384]{3,0,1,2:T(8,128)S(1)} %broadcast_select_fusion), channel_id=1, source_target_pairs={{0,2},{1,3},{2,4},{3,5},{4,6},{5,7},{6,8},{7,9},{8,10},{9,11},{10,... | collective-permute-start | bytes 3145736 | tf_op jit(solution)/shard_map/ppermute | solution.py:13
  103.6 108.2 %copy-start.3 = (s32[8,2]{0,1:T(2,128)S(1)}, s32[8,2]{0,1:T(2,128)}, u32[]{:S(2)}) copy-start(s32[8,2]{0,1:T(2,128)} %param.9) | copy-start | bytes 196
  103.7 24.3 %collective-permute-start.2 = (f32[8,2,1,16384]{3,0,1,2:T(8,128)S(1)}, f32[8,2,1,16384]{3,0,1,2:T(8,128)S(1)}, u32[]{:S(2)}, u32[]{:S(2)}) collective-permute-start(f32[8,2,1,16384]{3,0,1,2:T(8,128)S(1)} %broadcast_select_fusion.1), channel_id=1, source_target_pairs={{0,4},{1,5},{2,6},{3,7},{4,8},{5,9},{6,10},{7,11},{8,12},{9,13},{1... | collective-permute-start | bytes 3145736 | tf_op jit(solution)/shard_map/ppermute | solution.py:13
  128.2 117.9 %copy-start.2 = (f32[1,16384]{1,0:T(1,128)S(1)}, f32[1,16384]{1,0:T(1,128)}, u32[]{:S(2)}) copy-start(f32[1,16384]{1,0:T(1,128)} %param.10) | copy-start | bytes 196612
  128.2 48.8 %collective-permute-start.3 = (f32[8,2,1,16384]{3,0,1,2:T(8,128)S(1)}, f32[8,2,1,16384]{3,0,1,2:T(8,128)S(1)}, u32[]{:S(2)}, u32[]{:S(2)}) collective-permute-start(f32[8,2,1,16384]{3,0,1,2:T(8,128)S(1)} %broadcast_select_fusion.2), channel_id=1, source_target_pairs={{0,8},{1,9},{2,10},{3,11},{4,12},{5,13},{6,14},{7,15},{8,16},{9,17... | collective-permute-start | bytes 3145736 | tf_op jit(solution)/shard_map/ppermute | solution.py:13
  177.2 27.2 %collective-permute-start.4 = (f32[8,2,1,16384]{3,0,1,2:T(8,128)S(1)}, f32[8,2,1,16384]{3,0,1,2:T(8,128)S(1)}, u32[]{:S(2)}, u32[]{:S(2)}) collective-permute-start(f32[8,2,1,16384]{3,0,1,2:T(8,128)S(1)} %broadcast_select_fusion.3), channel_id=1, source_target_pairs={{0,16},{1,17},{2,18},{3,19},{4,20},{5,21},{6,22},{7,23},{8,24},{9,... | collective-permute-start | bytes 3145736 | tf_op jit(solution)/shard_map/ppermute | solution.py:13
  204.5 18.8 %collective-permute-start.6 = (f32[8,2,1,16384]{3,0,1,2:T(8,128)S(1)}, f32[8,2,1,16384]{3,0,1,2:T(8,128)S(1)}, u32[]{:S(2)}, u32[]{:S(2)}) collective-permute-start(f32[8,2,1,16384]{3,0,1,2:T(8,128)S(1)} %broadcast_select_fusion.4), channel_id=1, source_target_pairs={{1,0},{2,1},{3,2},{4,3},{5,4},{6,5},{7,6},{8,7},{9,8},{10,9},{11,1... | collective-permute-start | bytes 3145736 | tf_op jit(solution)/shard_map/ppermute | solution.py:24
  207.6 36.6 %collective-permute-start.5 = (f32[8,2,1,16384]{3,0,1,2:T(8,128)S(1)}, f32[8,2,1,16384]{3,0,1,2:T(8,128)}, u32[]{:S(2)}, u32[]{:S(2)}) collective-permute-start(f32[8,2,1,16384]{3,0,1,2:T(8,128)S(1)} %broadcast_select_fusion.4), channel_id=1, source_target_pairs={{0,1},{1,2},{2,3},{3,4},{4,5},{5,6},{6,7},{7,8},{8,9},{9,10},{10,1... | collective-permute-start | bytes 3145736 | tf_op jit(solution)/shard_map/ppermute | solution.py:23
  246.2 178.5 %copy-start = (f32[8,2,1,16384]{3,2,1,0:T(1,128)S(1)}, f32[8,2,1,16384]{3,2,1,0:T(1,128)}, u32[]{:S(2)}) copy-start(f32[8,2,1,16384]{3,2,1,0:T(1,128)} %param.11) | copy-start | bytes 3145732
Sparse Core Ops, SparseCore 0:
  255.5 169.1 reduce-scatter.1
